TPU v7x, 32 devices: a whole 2x2x4 slice. The times are simulated.
32 devices in a mesh: gx: 4 (over y, x), gy: 8 (over z, core).
Axes of the slice: x: 2, y: 2, z: 4, core: 2. Of those that a mesh axis runs over, the one named last changes fastest.
Arguments:
- grad_out: bfloat16 [16, 16, 64, 256], P('gx', 'gy'), may hold values from -6 to 6
- relu_mask: int32 [16, 16, 64, 256], P('gx', 'gy'), may hold values 0 or 1
- activations: bfloat16 [16, 16, 64, 256], P('gx', 'gy'), may hold values from -6 to 6
- weight: bfloat16 [27, 256, 256], P(None, 'gx'), may hold values from -0.078125 to 0.078125
Outputs:
- grad_input: bfloat16 [16, 16, 64, 256], P('gx', 'gy')
- weight_grad: float32 [27, 256, 256], P(None, 'gx', 'gy')
All inputs are finite; a program needn't handle non-finite values. No bound on the sum of `relu_mask` on one device may be relied on, other than what follows from the above.
Results may differ from a plain program's by a relative error of at most 0.001.
Values may be sent and summed in bfloat16 or wider, within the bound.
A program may use at most 64 MiB of HBM per device.

v0:
```python
import math

import jax
import jax.numpy as jnp
from jax import lax
from jax.sharding import PartitionSpec as P


def padded(shard, sides, width):
    for axis, dim in sides:
        devices, length = (lax.axis_size(axis), shard.shape[dim])
        up = [(i, (i + 1) % devices) for i in range(devices - 1)]
        down = [(j, i) for i, j in up]
        last = lax.slice_in_dim(shard, length - width, length, axis=dim)
        leading = lax.slice_in_dim(shard, 0, width, axis=dim)
        before = lax.ppermute(last, axis, up)
        after = lax.ppermute(leading, axis, down)
        shard = jnp.concatenate([before, shard, after], axis=dim)
    return shard


def tap_list():
    return [(a, b, c) for a in (-1, 0, 1) for b in (-1, 0, 1) for c in (-1, 0, 1)]


def body(grad_out, relu_mask, activations, weight):
    size_x, size_y, size_z = (grad_out.shape[0], grad_out.shape[1], grad_out.shape[2])
    out_chan = grad_out.shape[3]
    in_chan = activations.shape[3]
    cells = size_x * size_y * size_z
    gated = jnp.where(relu_mask != 0, grad_out, jnp.zeros_like(grad_out))
    grad_cycle = padded(gated, (("gx", 0), ("gy", 1)), 1)
    grad_pad = jnp.pad(grad_cycle, ((0, 0), (0, 0), (1, 1), (0, 0)))
    input_cycle = padded(activations, (("gx", 0), ("gy", 1)), 1)
    input_pad = jnp.pad(input_cycle, ((0, 0), (0, 0), (1, 1), (0, 0)))
    piece = lax.all_gather(weight, "gx", axis=1, tiled=True)
    accum = jnp.zeros((cells, piece.shape[1]), jnp.float32)
    for tap, (project_a, project_b, project_c) in enumerate(tap_list()):
        window = grad_pad[
            1 - project_a : 1 - project_a + size_x,
            1 - project_b : 1 - project_b + size_y,
            1 - project_c : 1 - project_c + size_z,
            :,
        ].reshape(cells, out_chan)
        accum = accum + lax.dot_general(
            window, piece[tap], (((1,), (1,)), ((), ())), preferred_element_type=jnp.float32
        )
    grad_input = accum.reshape(size_x, size_y, size_z, piece.shape[1]).astype(jnp.bfloat16)
    gated_flat = gated.reshape(cells, out_chan)
    terms = []
    for a, b, c in tap_list():
        shifted = input_pad[
            1 + a : 1 + a + size_x, 1 + b : 1 + b + size_y, 1 + c : 1 + c + size_z, :
        ].reshape(cells, in_chan)
        terms.append(
            lax.dot_general(
                shifted, gated_flat, (((0,), (0,)), ((), ())), preferred_element_type=jnp.float32
            )
        )
    partial_value = jnp.stack(terms, axis=0)[None]
    pieces = lax.all_to_all(partial_value, "gy", split_axis=3, concat_axis=0, tiled=True)
    section = jnp.sum(pieces, axis=0)
    summed = lax.psum_scatter(section, "gx", scatter_dimension=1, tiled=True)
    whole_cells = cells * lax.axis_size("gx") * lax.axis_size("gy")
    weight_grad = summed * (1.0 / math.sqrt(whole_cells))
    return (grad_input, weight_grad)


def solution(mesh):
    in_specs = (
        P("gx", "gy", None, None),
        P("gx", "gy", None, None),
        P("gx", "gy", None, None),
        P(None, "gx", None),
    )
    out_specs = (P("gx", "gy", None, None), P(None, "gx", "gy"))
    return jax.shard_map(body, mesh=mesh, in_specs=in_specs, out_specs=out_specs, check_vma=False)
```

profile of v0, /device:TPU:1, one launch (start us, length us, event | category | flops | bytes accessed | tf_op | source)
XLA Modules:
  0.0 301.5 jit_solution(12069150072496918049)
XLA Ops:
  8.0 3.9 %collective-permute-start.4 = (bf16[1,2,64,256]{3,2,1,0:T(8,128)(2,1)S(1)}, bf16[1,2,64,256]{3,2,1,0:T(8,128)(2,1)S(1)}, u32[]{:S(2)}, u32[]{:S(2)}) collective-permute-start(bf16[1,2,64,256]{3,2,1,0:T(8,128)(2,1)S(1)} %get-tuple-element.33), channel_id=1, source_target_pairs={{0,8},{8,16},{16,24},{1,9},{9,17},{17,25},{2,10},{10,18},{18,26},{... | collective-permute-start | bytes 196616 | tf_op jit(solution)/shard_map/ppermute | solution.py:16
  12.0 1.3 collective-permute-start.5
  14.3 2.7 collective-permute-done.5
  17.0 5.2 %collective-permute-start.6 = (bf16[6,1,64,256]{3,2,1,0:T(8,128)(2,1)S(1)}, bf16[6,1,64,256]{3,2,1,0:T(8,128)(2,1)S(1)}, u32[]{:S(2)}, u32[]{:S(2)}) collective-permute-start(bf16[6,1,64,256]{3,2,1,0:T(8,128)(2,1)S(1)} %get-tuple-element.26), channel_id=1, source_target_pairs={{0,1},{1,2},{2,3},{3,4},{4,5},{5,6},{6,7},{8,9},{9,10},{10,11},{11... | collective-permute-start | bytes 589832 | tf_op jit(solution)/shard_map/ppermute | solution.py:16
  22.3 2.1 collective-permute-start.7
  24.3 1.2 compare_select_fusion
  25.5 3.9 %collective-permute-done.7 = bf16[6,1,64,256]{3,2,1,0:T(8,128)(2,1)S(1)} collective-permute-done((bf16[6,1,64,256]{3,2,1,0:T(8,128)(2,1)S(1)}, bf16[6,1,64,256]{3,2,1,0:T(8,128)(2,1)S(1)}, u32[]{:S(2)}, u32[]{:S(2)}) %collective-permute-start.7) | collective-permute-done | bytes 196640 | tf_op jit(solution)/shard_map/ppermute | solution.py:17
  56.3 16.9 %copy.13 = f32[1,27,256,256]{2,0,1,3:T(1,128)} copy(f32[1,27,256,256]{3,2,1,0:T(8,128)} %bitcast.136) | data formatting | bytes 14155776 | tf_op jit(solution)/shard_map/broadcast_in_dim | solution.py:60
  73.2 4.8 %all-to-all-start = ((f32[1,27,256,256]{2,0,1,3:T(1,128)}), f32[1,27,256,256]{2,0,1,3:T(1,128)}, u32[]{:S(2)}, u32[]{:S(2)}) async-start(f32[1,27,256,256]{2,0,1,3:T(1,128)} %copy.13), calls=%async_computation | async-start | bytes 14155776 | tf_op jit(solution)/shard_map/all_to_all | solution.py:61
  78.8 4.0 %collective-permute-start = (bf16[1,2,64,256]{3,2,1,0:T(8,128)(2,1)S(1)}, bf16[1,2,64,256]{3,2,1,0:T(8,128)(2,1)S(1)}, u32[]{:S(2)}, u32[]{:S(2)}) collective-permute-start(bf16[1,2,64,256]{3,2,1,0:T(8,128)(2,1)S(1)} %get-tuple-element.36), channel_id=1, source_target_pairs={{0,8},{8,16},{16,24},{1,9},{9,17},{17,25},{2,10},{10,18},{18,26},{... | collective-permute-start | bytes 196616 | tf_op jit(solution)/shard_map/ppermute | solution.py:16
  82.8 1.3 collective-permute-start.1
  84.4 4.5 %collective-permute-done.1 = bf16[1,2,64,256]{3,2,1,0:T(8,128)(2,1)S(1)} collective-permute-done((bf16[1,2,64,256]{3,2,1,0:T(8,128)(2,1)S(1)}, bf16[1,2,64,256]{3,2,1,0:T(8,128)(2,1)S(1)}, u32[]{:S(2)}, u32[]{:S(2)}) %collective-permute-start.1) | collective-permute-done | bytes 65568 | tf_op jit(solution)/shard_map/ppermute | solution.py:17
  89.0 3.4 %collective-permute-start.2 = (bf16[6,1,64,256]{3,2,1,0:T(8,128)(2,1)S(1)}, bf16[6,1,64,256]{3,2,1,0:T(8,128)(2,1)S(1)}, u32[]{:S(2)}, u32[]{:S(2)}) collective-permute-start(bf16[6,1,64,256]{3,2,1,0:T(8,128)(2,1)S(1)} %get-tuple-element.30), channel_id=1, source_target_pairs={{0,1},{1,2},{2,3},{3,4},{4,5},{5,6},{6,7},{8,9},{9,10},{10,11},{11... | collective-permute-start | bytes 589832 | tf_op jit(solution)/shard_map/ppermute | solution.py:16
  92.4 2.1 collective-permute-start.3
  94.5 99.5 %collective-permute-done.2 = bf16[6,1,64,256]{3,2,1,0:T(8,128)(2,1)S(1)} collective-permute-done((bf16[6,1,64,256]{3,2,1,0:T(8,128)(2,1)S(1)}, bf16[6,1,64,256]{3,2,1,0:T(8,128)(2,1)S(1)}, u32[]{:S(2)}, u32[]{:S(2)}) %collective-permute-start.2) | collective-permute-done | bytes 196640 | tf_op jit(solution)/shard_map/ppermute | solution.py:16
  195.6 1.9 fusion.71
  197.5 1.3 fusion.62
  198.8 1.2 fusion.61
  200.0 1.3 convolution_add_fusion.23
  201.3 1.3 convolution_add_fusion.22
  207.1 26.1 %all-to-all-done = f32[1,27,256,256]{2,0,1,3:T(1,128)} async-done(((f32[1,27,256,256]{2,0,1,3:T(1,128)}), f32[1,27,256,256]{2,0,1,3:T(1,128)}, u32[]{:S(2)}, u32[]{:S(2)}) %all-to-all-start) | async-done | bytes 7077920 | tf_op jit(solution)/shard_map/all_to_all | solution.py:61
  233.2 6.8 %copy.14 = f32[1,27,256,256]{2,3,1,0:T(8,128)} copy(f32[1,27,256,256]{2,0,1,3:T(1,128)} %all-to-all-done) | data formatting | bytes 14155776 | tf_op jit(solution)/shard_map/all_to_all | solution.py:61
  240.0 3.9 %reduce_sum.9 = f32[27,256,32]{1,2,0:T(8,128)S(1)} reduce(f32[27,256,8,32]{1,3,2,0:T(8,128)} %bitcast.385, f32[]{:T(128)} %constant.2.clone.1), dimensions={2}, to_apply=%region_0.1 | reduce | flops 1548288 | bytes 7962628 | tf_op jit(solution)/shard_map/reduce_sum | solution.py:62
  244.0 4.4 %copy.43 = f32[27,256,32]{2,0,1:T(8,128)} copy(f32[27,256,32]{1,2,0:T(8,128)S(1)} %reduce_sum.9) | data formatting | bytes 1769472
  248.4 4.2 %reshape.170 = f32[256,864]{1,0:T(8,128)} reshape(f32[256,27,32]{2,1,0:T(8,128)} %bitcast.386) | data formatting | bytes 1769472
  254.9 1.2 convolution_add_fusion.4
  256.1 1.2 fusion.1
  257.2 1.2 convolution_add_fusion.2
  258.4 1.2 convolution_add_fusion.1
  259.6 1.9 fusion.3
  261.4 30.6 %reduce-scatter.4.cloned.1.call-done = f32[64,864]{1,0:T(8,128)} async-done(((f32[256,864]{1,0:T(8,128)}), f32[64,864]{1,0:T(8,128)}) %reduce-scatter.4.cloned.1.call-update) | async-done | bytes 221200
  292.0 1.3 reshape.171
  (97 shorter events, 39.4 us)
Async XLA Ops:
  8.0 5.3 %collective-permute-start.4 = (bf16[1,2,64,256]{3,2,1,0:T(8,128)(2,1)S(1)}, bf16[1,2,64,256]{3,2,1,0:T(8,128)(2,1)S(1)}, u32[]{:S(2)}, u32[]{:S(2)}) collective-permute-start(bf16[1,2,64,256]{3,2,1,0:T(8,128)(2,1)S(1)} %get-tuple-element.33), channel_id=1, source_target_pairs={{0,8},{8,16},{16,24},{1,9},{9,17},{17,25},{2,10},{10,18},{18,26},{... | collective-permute-start | bytes 196616 | tf_op jit(solution)/shard_map/ppermute | solution.py:16
  12.0 5.0 %collective-permute-start.5 = (bf16[1,2,64,256]{3,2,1,0:T(8,128)(2,1)S(1)}, bf16[1,2,64,256]{3,2,1,0:T(8,128)(2,1)S(1)}, u32[]{:S(2)}, u32[]{:S(2)}) collective-permute-start(bf16[1,2,64,256]{3,2,1,0:T(8,128)(2,1)S(1)} %get-tuple-element.32), channel_id=1, source_target_pairs={{8,0},{16,8},{24,16},{9,1},{17,9},{25,17},{10,2},{18,10},{26,18},{... | collective-permute-start | bytes 196616 | tf_op jit(solution)/shard_map/ppermute | solution.py:17
  17.0 8.5 %collective-permute-start.6 = (bf16[6,1,64,256]{3,2,1,0:T(8,128)(2,1)S(1)}, bf16[6,1,64,256]{3,2,1,0:T(8,128)(2,1)S(1)}, u32[]{:S(2)}, u32[]{:S(2)}) collective-permute-start(bf16[6,1,64,256]{3,2,1,0:T(8,128)(2,1)S(1)} %get-tuple-element.26), channel_id=1, source_target_pairs={{0,1},{1,2},{2,3},{3,4},{4,5},{5,6},{6,7},{8,9},{9,10},{10,11},{11... | collective-permute-start | bytes 589832 | tf_op jit(solution)/shard_map/ppermute | solution.py:16
  22.2 11.5 %copy-start.1 = (bf16[4,2,64,256]{3,2,1,0:T(8,128)(2,1)S(1)}, bf16[4,2,64,256]{3,2,1,0:T(8,128)(2,1)}, u32[]{:S(2)}) copy-start(bf16[4,2,64,256]{3,2,1,0:T(8,128)(2,1)} %param.6) | copy-start | bytes 786436
  22.3 7.1 %collective-permute-start.7 = (bf16[6,1,64,256]{3,2,1,0:T(8,128)(2,1)S(1)}, bf16[6,1,64,256]{3,2,1,0:T(8,128)(2,1)S(1)}, u32[]{:S(2)}, u32[]{:S(2)}) collective-permute-start(bf16[6,1,64,256]{3,2,1,0:T(8,128)(2,1)S(1)} %get-tuple-element.27), channel_id=1, source_target_pairs={{1,0},{2,1},{3,2},{4,3},{5,4},{6,5},{7,6},{9,8},{10,9},{11,10},{12... | collective-permute-start | bytes 589832 | tf_op jit(solution)/shard_map/ppermute | solution.py:17
  73.2 160.0 %all-to-all-start = ((f32[1,27,256,256]{2,0,1,3:T(1,128)}), f32[1,27,256,256]{2,0,1,3:T(1,128)}, u32[]{:S(2)}, u32[]{:S(2)}) async-start(f32[1,27,256,256]{2,0,1,3:T(1,128)} %copy.13), calls=%async_computation | async-start | bytes 14155776 | tf_op jit(solution)/shard_map/all_to_all | solution.py:61
  78.0 119.5 %all-gather.2.cloned.1.call-start = ((), (), s32[]{:S(2)}) async-start(), calls=%async_computation.2 | async-start | bytes 4423680 | tf_op jit(solution)/shard_map/all_gather | solution.py:36
  78.7 213.3 %reduce-scatter.4.cloned.1.call-start = ((), (), s32[]{:S(2)}) async-start(), calls=%async_computation.3 | async-start | bytes 1146880
  78.8 5.6 %collective-permute-start = (bf16[1,2,64,256]{3,2,1,0:T(8,128)(2,1)S(1)}, bf16[1,2,64,256]{3,2,1,0:T(8,128)(2,1)S(1)}, u32[]{:S(2)}, u32[]{:S(2)}) collective-permute-start(bf16[1,2,64,256]{3,2,1,0:T(8,128)(2,1)S(1)} %get-tuple-element.36), channel_id=1, source_target_pairs={{0,8},{8,16},{16,24},{1,9},{9,17},{17,25},{2,10},{10,18},{18,26},{... | collective-permute-start | bytes 196616 | tf_op jit(solution)/shard_map/ppermute | solution.py:16
  82.8 6.1 %collective-permute-start.1 = (bf16[1,2,64,256]{3,2,1,0:T(8,128)(2,1)S(1)}, bf16[1,2,64,256]{3,2,1,0:T(8,128)(2,1)S(1)}, u32[]{:S(2)}, u32[]{:S(2)}) collective-permute-start(bf16[1,2,64,256]{3,2,1,0:T(8,128)(2,1)S(1)} %get-tuple-element.37), channel_id=1, source_target_pairs={{8,0},{16,8},{24,16},{9,1},{17,9},{25,17},{10,2},{18,10},{26,18},{... | collective-permute-start | bytes 196616 | tf_op jit(solution)/shard_map/ppermute | solution.py:17
  89.0 105.1 %collective-permute-start.2 = (bf16[6,1,64,256]{3,2,1,0:T(8,128)(2,1)S(1)}, bf16[6,1,64,256]{3,2,1,0:T(8,128)(2,1)S(1)}, u32[]{:S(2)}, u32[]{:S(2)}) collective-permute-start(bf16[6,1,64,256]{3,2,1,0:T(8,128)(2,1)S(1)} %get-tuple-element.30), channel_id=1, source_target_pairs={{0,1},{1,2},{2,3},{3,4},{4,5},{5,6},{6,7},{8,9},{9,10},{10,11},{11... | collective-permute-start | bytes 589832 | tf_op jit(solution)/shard_map/ppermute | solution.py:16
  92.4 101.6 %collective-permute-start.3 = (bf16[6,1,64,256]{3,2,1,0:T(8,128)(2,1)S(1)}, bf16[6,1,64,256]{3,2,1,0:T(8,128)(2,1)S(1)}, u32[]{:S(2)}, u32[]{:S(2)}) collective-permute-start(bf16[6,1,64,256]{3,2,1,0:T(8,128)(2,1)S(1)} %get-tuple-element.31), channel_id=1, source_target_pairs={{1,0},{2,1},{3,2},{4,3},{5,4},{6,5},{7,6},{9,8},{10,9},{11,10},{12... | collective-permute-start | bytes 589832 | tf_op jit(solution)/shard_map/ppermute | solution.py:17
  197.5 5.1 %copy-start = (bf16[27,256,256]{2,1,0:T(8,128)(2,1)S(1)}, bf16[27,256,256]{2,1,0:T(8,128)(2,1)}, u32[]{:S(2)}) copy-start(bf16[27,256,256]{2,1,0:T(8,128)(2,1)} %all-gather.2.cloned.1.call-done) | copy-start | bytes 10616836
  197.5 5.1 %copy-start.13 = (bf16[4,2,64,256]{3,2,1,0:T(8,128)(2,1)S(1)}, bf16[4,2,64,256]{3,2,1,0:T(8,128)(2,1)}, u32[]{:S(2)}) copy-start(bf16[4,2,64,256]{3,2,1,0:T(8,128)(2,1)} %get-tuple-element.17) | copy-start | bytes 786436
  198.8 4.4 %copy-start.12 = (bf16[4,2,64,256]{3,2,1,0:T(8,128)(2,1)S(1)}, bf16[4,2,64,256]{3,2,1,0:T(8,128)(2,1)}, u32[]{:S(2)}) copy-start(bf16[4,2,64,256]{3,2,1,0:T(8,128)(2,1)} %get-tuple-element.15) | copy-start | bytes 786436
  200.0 3.5 %copy-start.7 = (bf16[4,2,64,256]{3,2,1,0:T(8,128)(2,1)S(1)}, bf16[4,2,64,256]{3,2,1,0:T(8,128)(2,1)}, u32[]{:S(2)}) copy-start(bf16[4,2,64,256]{3,2,1,0:T(8,128)(2,1)} %get-tuple-element.22) | copy-start | bytes 786436
  201.3 2.4 copy-start.11
  202.6 1.4 copy-start.10
  202.9 1.4 copy-start.4
  203.2 1.4 copy-start.9
  203.5 1.4 copy-start.8
  204.0 1.4 copy-start.6
  204.3 1.4 copy-start.5
  204.9 1.4 copy-start.3
  205.2 1.4 copy-start.2
Sparse Core Ops, SparseCore 0:
  80.6 46.8 all-gather.1
  252.7 39.2 reduce-scatter.3
where the time goes:
time: 304 us; the launch traced here: 302 us
  waiting for transfers between devices  168 us (55%)
  matrix products  44.5 us (15%)
  local copies, waits for them, and re-layouts  39 us (13%)
  starting transfers between devices  28.2 us (9%)
  between operations  14.6 us (5%)
  other arithmetic  7.02 us (2%)
    ppermute x4, waiting for transfers between devices, padded(): before = lax.ppermute(last, axis, up)  99.8 us
    unnamed x3, waiting for transfers between devices  31.3 us
    dot_general x27, matrix products, body(): lax.dot_general(shifted, gated_flat, (((0,), (0,)), ((), ())), preferred_...  26.5 us
    all_to_all x1, waiting for transfers between devices, body(): lax.all_to_all(partial_value, 'gy', split_axis=3, concat_axis=0, tiled=True)  26.1 us
    dot_general x27, matrix products, body(): lax.dot_general(window, piece[tap], (((1,), (1,)), ((), ())), preferred_e...  18.1 us
    broadcast_in_dim x1, local copies, waits for them, and re-layouts, body(): partial_value = jnp.stack(terms, axis=0)[None]  16.9 us
    ppermute x4, starting transfers between devices, padded(): before = lax.ppermute(last, axis, up)  16.6 us
    unnamed x34, local copies, waits for them, and re-layouts  11.5 us
  transfers between devices with their start and end apart: 11, of which 7 were waited for; matrix products, arithmetic and copies ran while one was open for 8% of the time, Pallas kernels for 0%

commit v1 on v0

v1 whole, which is shorter than its diff:
```python
import functools
import math

import jax
import jax.numpy as jnp
from jax import lax
from jax.experimental import pallas as pl
from jax.experimental.pallas import tpu as pltpu
from jax.sharding import PartitionSpec as P

MESH = pl.DeviceIdType.MESH
ORDER = (1, 4, 7, 0, 3, 6, 2, 5, 8)
PER = 2


def kernel(nx, ny, scale, gated_ref, act_ref, w_ref, out_ref, wg_ref,
           gbuf, abuf, a3, wbuf, acc, dwt, pair, red, rs, gsend, grecv,
           loc_sem, gat_s, gat_r, act_s, act_r, halo_s, halo_r,
           pair_s, pair_r, rs_s, rs_r, gi_s, gi_r):
    g = lax.axis_index("gx")
    h = lax.axis_index("gy")
    sx, sy, sz, co = gated_ref.shape
    ish = w_ref.shape[1]
    rows = 3 * ish
    cells = sx * sy * sz
    nz = ny // 2
    z = h // 2
    core = h - 2 * z
    partner = 2 * z + 1 - core
    chunks = [ORDER[i:i + PER] for i in range(0, 9, PER)]

    def xpeer(s):
        return lax.rem(g + s, nx)

    def xfrom(s):
        return lax.rem(g + nx - s, nx)

    def zpeer(s):
        return 2 * lax.rem(z + s, nz) + core

    barrier = pltpu.get_barrier_semaphore()
    for s in range(1, nx):
        pl.semaphore_signal(barrier, inc=1, device_id=(xpeer(s), h), device_id_type=MESH)
    for s in range(1, nz):
        pl.semaphore_signal(barrier, inc=1, device_id=(g, zpeer(s)), device_id_type=MESH)
    pl.semaphore_signal(barrier, inc=1, device_id=(g, partner), device_id_type=MESH)
    outer = h + 2 * core - 1
    has_outer = jnp.logical_and(outer >= 0, outer < ny)

    @pl.when(has_outer)
    def _():
        pl.semaphore_signal(barrier, inc=1, device_id=(g, outer), device_id_type=MESH)

    mine = gbuf.at[pl.ds(1 + sx * g, sx), pl.ds(1, sy)]
    own_g = pltpu.make_async_copy(gated_ref, mine, loc_sem.at[0])
    own_a = pltpu.make_async_copy(act_ref.at[g], abuf.at[g], loc_sem.at[1])
    own_w = pltpu.make_async_copy(w_ref, wbuf, loc_sem.at[2])
    own_g.start()
    own_a.start()
    own_w.start()
    gbuf[0] = jnp.zeros(gbuf.shape[1:], gbuf.dtype)
    gbuf[sx * nx + 1] = jnp.zeros(gbuf.shape[1:], gbuf.dtype)

    @pl.when(h == 0)
    def _():
        gbuf[pl.ds(1, sx * nx), 0] = jnp.zeros((sx * nx, sz, co), gbuf.dtype)

    @pl.when(h == ny - 1)
    def _():
        gbuf[pl.ds(1, sx * nx), sy + 1] = jnp.zeros((sx * nx, sz, co), gbuf.dtype)

    pl.semaphore_wait(barrier, nx - 1 + nz - 1 + 1 + has_outer.astype(jnp.int32))

    gat = {}
    acts = {}
    for s in range(1, nx):
        gat[s] = pltpu.make_async_remote_copy(
            src_ref=gated_ref, dst_ref=mine, send_sem=gat_s.at[s], recv_sem=gat_r.at[s],
            device_id=(xpeer(s), h), device_id_type=MESH)
        gat[s].start()
    for s in range(1, nx):
        acts[s] = pltpu.make_async_remote_copy(
            src_ref=act_ref.at[xpeer(s)], dst_ref=abuf.at[g], send_sem=act_s.at[s],
            recv_sem=act_r.at[s], device_id=(xpeer(s), h), device_id_type=MESH)
        acts[s].start()

    def halo(s, up):
        block = pl.ds(1 + sx * xfrom(s), sx)
        src = gbuf.at[block, sy] if up else gbuf.at[block, 1]
        dst = gbuf.at[block, 0] if up else gbuf.at[block, sy + 1]
        k = 0 if up else 1
        return pltpu.make_async_remote_copy(
            src_ref=src, dst_ref=dst, send_sem=halo_s.at[k, s], recv_sem=halo_r.at[k, s],
            device_id=(g, h + 1 if up else h - 1), device_id_type=MESH)

    own_g.wait()
    for s in range(nx):
        if s > 0:
            gat[s].wait_recv()

        @pl.when(h < ny - 1)
        def _():
            halo(s, True).start()

        @pl.when(h > 0)
        def _():
            halo(s, False).start()

    lane = lax.broadcasted_iota(jnp.int32, (ish, cells), 1)
    zpos = lax.rem(lane, sz)
    own_a.wait()
    for s in range(nx):
        if s > 0:
            acts[s].wait_recv()
        p = xfrom(s)
        v = abuf[p].astype(jnp.float32)
        a3[p, pl.ds(0, ish)] = jnp.where(
            zpos >= 1, pltpu.roll(v, 1, 1), 0.0).astype(jnp.bfloat16)
        a3[p, pl.ds(ish, ish)] = v.astype(jnp.bfloat16)
        a3[p, pl.ds(2 * ish, ish)] = jnp.where(
            zpos <= sz - 2, pltpu.roll(v, cells - 1, 1), 0.0).astype(jnp.bfloat16)
    own_w.wait()

    def window(ab, p):
        a = ab // 3 - 1
        b = ab - 3 * (ab // 3) - 1
        return gbuf[pl.ds(1 - a + sx * p, sx), pl.ds(1 - b, sy)].reshape(cells, co)

    def pair_copy(k, width):
        return pltpu.make_async_remote_copy(
            src_ref=dwt.at[k, :, 1 - core, :, pl.ds(0, width)],
            dst_ref=pair.at[k, :, :, pl.ds(0, width)],
            send_sem=pair_s.at[k], recv_sem=pair_r.at[k],
            device_id=(g, partner), device_id_type=MESH)

    def rs_copy(k, s, width):
        return pltpu.make_async_remote_copy(
            src_ref=red.at[k, lax.rem(z + s, nz), :, pl.ds(0, width)],
            dst_ref=rs.at[k, s, :, pl.ds(0, width)],
            send_sem=rs_s.at[k, s], recv_sem=rs_r.at[k, s],
            device_id=(g, zpeer(s)), device_id_type=MESH)

    widths = [-(-len(c) * rows // 128) * 128 for c in chunks]

    def finish_pair(k):
        w = widths[k]
        pair_copy(k, w).wait_recv()
        red[k, :, :, pl.ds(0, w)] = dwt[k, :, core, :, pl.ds(0, w)] + pair[k, :, :, pl.ds(0, w)]
        for s in range(1, nz):
            rs_copy(k, s, w).start()

    seen_halo = False
    for k, chunk in enumerate(chunks):
        for j, ab in enumerate(chunk):
            if ab % 3 != 1 and not seen_halo:
                seen_halo = True

                @pl.when(h > 0)
                def _():
                    for s in range(nx):
                        halo(s, True).wait_recv()

                @pl.when(h < ny - 1)
                def _():
                    for s in range(nx):
                        halo(s, False).wait_recv()

            def step(p, total, ab=ab):
                return total + jnp.dot(a3[p], window(ab, p), preferred_element_type=jnp.float32)
            total = lax.fori_loop(
                0, nx, step, jnp.zeros((rows, co), jnp.float32), unroll=nx <= 4)
            acc[k, pl.ds(j * rows, rows)] = total
        used = len(chunk) * rows
        if used < widths[k]:
            acc[k, pl.ds(used, widths[k] - used)] = jnp.zeros((widths[k] - used, co), jnp.float32)
        w = widths[k]
        dwt[k, :, :, :, pl.ds(0, w)] = acc[k, pl.ds(0, w)].T.reshape(nz, 2, co // ny, w)
        pair_copy(k, w).start()
        if k > 0:
            finish_pair(k - 1)
    finish_pair(len(chunks) - 1)

    def gi_copy(s):
        return pltpu.make_async_remote_copy(
            src_ref=gsend.at[s], dst_ref=grecv.at[g], send_sem=gi_s.at[s], recv_sem=gi_r.at[s],
            device_id=(xpeer(s), h), device_id_type=MESH)

    def shifted(p):
        def step(ab, total):
            return total + lax.dot_general(
                wbuf[pl.ds(3 * ab, 3)].reshape(rows, co), window(ab, p),
                (((1,), (1,)), ((), ())), preferred_element_type=jnp.float32)
        prod = lax.fori_loop(0, 9, step, jnp.zeros((rows, cells), jnp.float32))
        low = jnp.where(zpos <= sz - 2, pltpu.roll(prod[:ish], cells - 1, 1), 0.0)
        high = jnp.where(zpos >= 1, pltpu.roll(prod[2 * ish:], 1, 1), 0.0)
        return (prod[ish:2 * ish] + low + high).astype(jnp.bfloat16)

    for s in range(1, nx):
        gsend[s] = shifted(xpeer(s))
        gi_copy(s).start()
    grecv[g] = shifted(g)

    for s in range(1, nx):
        gi_copy(s).wait_recv()
    full = grecv[...].reshape(nx * ish, cells).astype(jnp.float32)
    out_ref[...] = full.T.astype(jnp.bfloat16).reshape(sx, sy, sz, nx * ish)
    for k, chunk in enumerate(chunks):
        w = widths[k]
        total = red[k, z, :, pl.ds(0, w)]
        for s in range(1, nz):
            rs_copy(k, s, w).wait_recv()
            total = total + rs[k, s, :, pl.ds(0, w)]
        block = (total * scale).T
        for j, ab in enumerate(chunk):
            wg_ref[pl.ds(3 * ab, 3)] = block[j * rows:(j + 1) * rows].reshape(3, ish, co // ny)

    for s in range(1, nx):
        gat[s].wait_send()
        acts[s].wait_send()
        gi_copy(s).wait_send()

    @pl.when(h < ny - 1)
    def _():
        for s in range(nx):
            halo(s, True).wait_send()

    @pl.when(h > 0)
    def _():
        for s in range(nx):
            halo(s, False).wait_send()

    for k in range(len(chunks)):
        pair_copy(k, widths[k]).wait_send()
        for s in range(1, nz):
            rs_copy(k, s, widths[k]).wait_send()


def body(nx, ny, grad_out, relu_mask, activations, weight):
    sx, sy, sz, co = grad_out.shape
    ish = weight.shape[1]
    rows = 3 * ish
    cells = sx * sy * sz
    nz = ny // 2
    nch = -(-9 // PER)
    wide = -(-PER * rows // 128) * 128
    gated = jnp.where(relu_mask != 0, grad_out, jnp.zeros_like(grad_out))
    act_t = activations.reshape(cells, nx * ish).T.reshape(nx, ish, cells)
    scale = 1.0 / math.sqrt(cells * nx * ny)
    dma = pltpu.SemaphoreType.DMA
    bf, f32 = jnp.bfloat16, jnp.float32
    any_spec = pl.BlockSpec(memory_space=pl.ANY)
    vmem_spec = pl.BlockSpec(memory_space=pltpu.VMEM)
    out, wg = pl.pallas_call(
        functools.partial(kernel, nx, ny, scale),
        out_shape=(jax.ShapeDtypeStruct((sx, sy, sz, nx * ish), bf),
                   jax.ShapeDtypeStruct((27, ish, co // ny), f32)),
        in_specs=[any_spec] * 3,
        out_specs=(vmem_spec, vmem_spec),
        scratch_shapes=[
            pltpu.VMEM((sx * nx + 2, sy + 2, sz, co), bf),
            pltpu.VMEM((nx, ish, cells), bf),
            pltpu.VMEM((nx, rows, cells), bf),
            pltpu.VMEM((27, ish, co), bf),
            pltpu.VMEM((nch, wide, co), f32),
            pltpu.VMEM((nch, nz, 2, co // ny, wide), f32),
            pltpu.VMEM((nch, nz, co // ny, wide), f32),
            pltpu.VMEM((nch, nz, co // ny, wide), f32),
            pltpu.VMEM((nch, nz, co // ny, wide), f32),
            pltpu.VMEM((nx, ish, cells), bf),
            pltpu.VMEM((nx, ish, cells), bf),
            dma((3,)), dma((nx,)), dma((nx,)), dma((nx,)), dma((nx,)),
            dma((2, nx)), dma((2, nx)), dma((nch,)), dma((nch,)),
            dma((nch, nz)), dma((nch, nz)), dma((nx,)), dma((nx,)),
        ],
        compiler_params=pltpu.CompilerParams(
            collective_id=0, has_side_effects=True, vmem_limit_bytes=60 * 1024 * 1024),
        name="conv_backward",
    )(gated, act_t, weight)
    return out, wg


def solution(mesh):
    nx, ny = mesh.shape["gx"], mesh.shape["gy"]
    in_specs = (
        P("gx", "gy", None, None),
        P("gx", "gy", None, None),
        P("gx", "gy", None, None),
        P(None, "gx", None),
    )
    out_specs = (P("gx", "gy", None, None), P(None, "gx", "gy"))
    return jax.shard_map(
        functools.partial(body, nx, ny), mesh=mesh, in_specs=in_specs, out_specs=out_specs,
        check_vma=False)
```

time: 304 us -> 53.6 us (0.18)
  waiting for transfers between devices: 168 us -> 0 us
  Pallas kernels: 0 us -> 46.7 us
  matrix products: 44.5 us -> 0 us
  local copies, waits for them, and re-layouts: 39 us -> 3.82 us
  starting transfers between devices: 28.2 us -> 0 us
  between operations: 14.6 us -> 0.66 us
  other arithmetic: 7.02 us -> 1.93 us
    ppermute x8 -> x0, waiting for transfers between devices: 111 us -> none  [the longest x4 99.8 us: padded(): before = lax.ppermute(last, axis, up)]
    pallas_call x0 -> x1, Pallas kernels: none -> 46.7 us  [body(): pl.pallas_call(functools.partial(kernel, nx, ny, scale), out_shape=(jax.S...]
    dot_general x54 -> x0, matrix products: 44.5 us -> none  [the longest x27 26.5 us: body(): lax.dot_general(shifted, gated_flat, (((0,), (0,)), ((), ())), preferred_...]
    unnamed x3 -> x0, waiting for transfers between devices: 31.3 us -> none
    all_to_all x1 -> x0, waiting for transfers between devices: 26.1 us -> none  [body(): lax.all_to_all(partial_value, 'gy', split_axis=3, concat_axis=0, tiled=True)]
    ppermute x8 -> x0, starting transfers between devices: 23.3 us -> none  [the longest x4 16.6 us: padded(): before = lax.ppermute(last, axis, up)]
    broadcast_in_dim x1 -> x0, local copies, waits for them, and re-layouts: 16.9 us -> none  [body(): partial_value = jnp.stack(terms, axis=0)[None]]
    unnamed x34 -> x5, local copies, waits for them, and re-layouts: 11.5 us -> 0.71 us
  transfers between devices with their start and end apart: 11 -> 0, of which waited for: 7 -> 0; matrix products, arithmetic and copies ran while one was open for 8% -> 0% of each run, Pallas kernels for 0% -> 0%
where the time goes in v1:
time: 53.6 us; the launch traced here: 53.1 us
  Pallas kernels  46.7 us (87%)
  local copies, waits for them, and re-layouts  3.82 us (7%)
  other arithmetic  1.93 us (4%)
  between operations  0.66 us (1%)
    pallas_call x1, Pallas kernels, body(): pl.pallas_call(functools.partial(kernel, nx, ny, scale), out_shape=(jax.S...  46.7 us
    pallas_call x1, local copies, waits for them, and re-layouts, body(): pl.pallas_call(functools.partial(kernel, nx, ny, scale), out_shape=(jax.S...  2.26 us
    select_n x1, other arithmetic, body(): gated = jnp.where(relu_mask != 0, grad_out, jnp.zeros_like(grad_out))  1.93 us

profile of v1, /device:TPU:1, one launch (start us, length us, event | category | flops | bytes accessed | tf_op | source)
XLA Modules:
  0.0 53.1 jit_solution(1138461975629547457)
XLA Ops:
  0.6 0.0 copy-start
  0.6 1.9 %compare_select_fusion.gated_ref = bf16[4,2,64,256]{3,2,1,0:T(8,128)(2,1)} fusion(bf16[4,2,64,256]{3,2,1,0:T(8,128)(2,1)} %param.4, s32[4,2,64,256]{3,2,1,0:T(8,128)} %param.5), kind=kLoop, calls=%fused_computation | loop fusion | flops 262144 | bytes 1048576 | tf_op jit(solution)/shard_map/jit(_where)/select_n | solution.py:246
  2.6 0.0 copy-done
  2.6 0.8 %copy.6 = bf16[512,256]{0,1:T(8,128)(2,1)} copy(bf16[512,256]{1,0:T(8,128)(2,1)S(1)} %bitcast.5) | data formatting | bytes 524288 | tf_op jit(solution)/shard_map/reshape | solution.py:247
  3.4 46.7 %conv_backward.1 = (bf16[4,2,64,256]{3,2,1,0:T(8,128)(2,1)}, f32[27,64,32]{2,1,0:T(8,128)}) custom-call(bf16[4,2,64,256]{3,2,1,0:T(8,128)(2,1)} %compare_select_fusion.gated_ref, bf16[4,64,512]{2,1,0:T(8,128)(2,1)} %bitcast.4, bf16[27,64,256]{2,1,0:T(8,128)(2,1)} %w_ref.1), custom_call_target="tpu_custom_call" | custom-call | tf_op jit(solution)/shard_map/conv_backward/pallas_call | solution.py:253
  50.1 0.0 copy-start.1
  50.1 2.3 %copy.7 = f32[27,64,32]{1,2,0:T(8,128)} copy(f32[27,64,32]{2,1,0:T(8,128)} %get-tuple-element.3) | data formatting | bytes 442368 | tf_op jit(solution)/shard_map/conv_backward/pallas_call | solution.py:253
  52.3 0.0 copy-done.1
  52.4 0.7 %copy.9 = bf16[4,2,64,256]{3,2,1,0:T(8,128)(2,1)} copy(bf16[4,2,64,256]{3,2,1,0:T(8,128)(2,1)S(1)} %copy-done.1) | data formatting | bytes 524288
Async XLA Ops:
  0.6 1.9 %copy-start = (bf16[4,2,64,256]{3,2,1,0:T(8,128)(2,1)S(1)}, bf16[4,2,64,256]{3,2,1,0:T(8,128)(2,1)}, u32[]{:S(2)}) copy-start(bf16[4,2,64,256]{3,2,1,0:T(8,128)(2,1)} %param.6) | copy-start | bytes 786436
  50.1 2.3 %copy-start.1 = (bf16[4,2,64,256]{3,2,1,0:T(8,128)(2,1)S(1)}, bf16[4,2,64,256]{3,2,1,0:T(8,128)(2,1)}, u32[]{:S(2)}) copy-start(bf16[4,2,64,256]{3,2,1,0:T(8,128)(2,1)} %get-tuple-element.6) | copy-start | bytes 786436

commit v2 on v0

v2 whole, which is shorter than its diff:
```python
import functools
import math

import jax
import jax.numpy as jnp
from jax import lax
from jax.experimental import pallas as pl
from jax.experimental.pallas import tpu as pltpu
from jax.sharding import PartitionSpec as P

MESH = pl.DeviceIdType.MESH
ORDER = (1, 4, 7, 0, 3, 6, 2, 5, 8)
PER = 2
CHUNKS = [ORDER[i:i + PER] for i in range(0, 9, PER)]
NCH = len(CHUNKS)
LAG = 2


def kernel(nx, ny, nbits, scale, *refs):
    (grad_ref, mask_ref, act_ref, w_ref, out_ref, wg_ref,
     gin, min_, ain, gbuf, asend, abuf, a3, wbuf, wp, acc, dwt, pair, gsend, grecv) = refs[:20]
    curs = refs[20:20 + nbits - 1]
    recvs = refs[20 + nbits - 1:20 + 2 * (nbits - 1)]
    (loc_sem, gat_s, gat_r, act_s, act_r, halo_s, halo_r,
     pair_s, pair_r, rs_s, rs_r, gi_s, gi_r) = refs[20 + 2 * (nbits - 1):]
    g = lax.axis_index("gx")
    h = lax.axis_index("gy")
    sx, sy, sz, co = gin.shape
    ish = w_ref.shape[1]
    osh = co // ny
    hc = co // 2
    rows = 3 * ish
    cells = sx * sy * sz
    f32, bf = jnp.float32, jnp.bfloat16
    core = lax.rem(h, 2)
    bits = [lax.rem(h // 2 ** j, 2) for j in range(nbits)]
    partners = [h + 2 ** j * (1 - 2 * bits[j]) for j in range(nbits)]

    def xpeer(s):
        return lax.rem(g + s, nx)

    def xfrom(s):
        return lax.rem(g + nx - s, nx)

    in_g = pltpu.make_async_copy(grad_ref, gin, loc_sem.at[0])
    in_m = pltpu.make_async_copy(mask_ref, min_, loc_sem.at[1])
    in_a = pltpu.make_async_copy(act_ref, ain, loc_sem.at[2])
    in_w = pltpu.make_async_copy(w_ref, wbuf, loc_sem.at[3])
    in_m.start()
    in_g.start()
    in_a.start()
    in_w.start()

    barrier = pltpu.get_barrier_semaphore()
    for s in range(1, nx):
        pl.semaphore_signal(barrier, inc=1, device_id=(xpeer(s), h), device_id_type=MESH)
    for j in range(nbits):
        pl.semaphore_signal(barrier, inc=1, device_id=(g, partners[j]), device_id_type=MESH)
    outer = h + 2 * core - 1
    has_outer = jnp.logical_and(outer >= 0, outer < ny)

    @pl.when(has_outer)
    def _():
        pl.semaphore_signal(barrier, inc=1, device_id=(g, outer), device_id_type=MESH)

    o_in = lax.broadcasted_iota(jnp.int32, (co, co), 0)
    o_out = lax.broadcasted_iota(jnp.int32, (co, co), 1)
    owner = lax.div(o_in, osh)
    place = lax.rem(owner, 2) * hc + lax.div(owner, 2) * osh + lax.rem(o_in, osh)
    perm = jnp.where(place == o_out, 1.0, 0.0).astype(bf)

    in_m.wait()
    in_g.wait()
    gated = jnp.where(min_[...].reshape(cells, co) != 0,
                      gin[...].reshape(cells, co).astype(f32), 0.0).astype(bf)
    ordered = jnp.dot(gated, perm, preferred_element_type=f32).astype(bf)
    mine = (pl.ds(1 + sx * g, sx), pl.ds(1, sy))
    for q in range(2):
        gbuf[(q,) + mine] = ordered[:, q * hc:(q + 1) * hc].reshape(sx, sy, sz, hc)
    in_a.wait()
    asend[...] = ain[...].reshape(cells, nx * ish).astype(f32).T.astype(bf).reshape(
        nx, ish, cells)

    pl.semaphore_wait(barrier, nx - 1 + nbits + has_outer.astype(jnp.int32))

    gat = {}
    acts = {}
    for s in range(1, nx):
        acts[s] = pltpu.make_async_remote_copy(
            src_ref=asend.at[xpeer(s)], dst_ref=abuf.at[g], send_sem=act_s.at[s],
            recv_sem=act_r.at[s], device_id=(xpeer(s), h), device_id_type=MESH)
        acts[s].start()
    for q in range(2):
        for s in range(1, nx):
            gat[q, s] = pltpu.make_async_remote_copy(
                src_ref=gbuf.at[(q,) + mine], dst_ref=gbuf.at[(q,) + mine],
                send_sem=gat_s.at[q, s], recv_sem=gat_r.at[q, s],
                device_id=(xpeer(s), h), device_id_type=MESH)
            gat[q, s].start()

    def halo(q, s, up):
        block = pl.ds(1 + sx * xfrom(s), sx)
        src = gbuf.at[q, block, sy] if up else gbuf.at[q, block, 1]
        dst = gbuf.at[q, block, 0] if up else gbuf.at[q, block, sy + 1]
        k = 0 if up else 1
        return pltpu.make_async_remote_copy(
            src_ref=src, dst_ref=dst, send_sem=halo_s.at[q, k, s], recv_sem=halo_r.at[q, k, s],
            device_id=(g, h + 1 if up else h - 1), device_id_type=MESH)

    def forward(q, s):
        @pl.when(h < ny - 1)
        def _():
            halo(q, s, True).start()

        @pl.when(h > 0)
        def _():
            halo(q, s, False).start()

    forward(0, 0)
    forward(1, 0)
    for q in range(2):
        gbuf[q, 0] = jnp.zeros((sy + 2, sz, hc), bf)
        gbuf[q, sx * nx + 1] = jnp.zeros((sy + 2, sz, hc), bf)

        @pl.when(h == 0)
        def _():
            gbuf[q, pl.ds(1, sx * nx), 0] = jnp.zeros((sx * nx, sz, hc), bf)

        @pl.when(h == ny - 1)
        def _():
            gbuf[q, pl.ds(1, sx * nx), sy + 1] = jnp.zeros((sx * nx, sz, hc), bf)

    in_w.wait()
    wp[...] = jnp.dot(wbuf[...].reshape(27 * ish, co), perm,
                      preferred_element_type=f32).astype(bf).reshape(27, ish, co)

    zpos = lax.rem(lax.broadcasted_iota(jnp.int32, (ish, cells), 1), sz)

    def spread(p, v):
        v = v.astype(f32)
        a3[p, pl.ds(0, ish)] = jnp.where(zpos >= 1, pltpu.roll(v, 1, 1), 0.0).astype(bf)
        a3[p, pl.ds(ish, ish)] = v.astype(bf)
        a3[p, pl.ds(2 * ish, ish)] = jnp.where(
            zpos <= sz - 2, pltpu.roll(v, cells - 1, 1), 0.0).astype(bf)

    spread(g, asend[g])
    for s in range(1, nx):
        acts[s].wait_recv()
        spread(xfrom(s), abuf[xfrom(s)])

    def window(q, ab, p):
        a = ab // 3 - 1
        b = ab - 3 * (ab // 3) - 1
        return gbuf[q, pl.ds(1 - a + sx * p, sx), pl.ds(1 - b, sy)].reshape(cells, hc)

    widths = [-(-len(c) * rows // 128) * 128 for c in CHUNKS]
    steps = [(q, k) for q in range(2) for k in range(NCH)]

    def pair_copy(q, k):
        w = widths[k]
        return pltpu.make_async_remote_copy(
            src_ref=dwt.at[q, k, :, :, pl.ds(0, w)], dst_ref=pair.at[k, :, :, pl.ds(0, w)],
            send_sem=pair_s.at[k], recv_sem=pair_r.at[k],
            device_id=(g, partners[0]), device_id_type=MESH)

    def stage_copy(k, j):
        w = widths[k]
        return pltpu.make_async_remote_copy(
            src_ref=curs[j - 1].at[k, :, 1 - bits[j], :, pl.ds(0, w)],
            dst_ref=recvs[j - 1].at[k, :, :, pl.ds(0, w)],
            send_sem=rs_s.at[k, j], recv_sem=rs_r.at[k, j],
            device_id=(g, partners[j]), device_id_type=MESH)

    def arrived(q, k, j):
        w = widths[k]
        if j == 0:
            pair_copy(q, k).wait_recv()
            return dwt[q, k, :, :, pl.ds(0, w)] + pair[k, :, :, pl.ds(0, w)]
        stage_copy(k, j).wait_recv()
        return (curs[j - 1][k, :, bits[j], :, pl.ds(0, w)]
                + recvs[j - 1][k, :, :, pl.ds(0, w)])

    def advance(q, k, j):
        @pl.when(core == q)
        def _():
            total = arrived(q, k, j)
            n = total.shape[0]
            curs[j][k, :, :, :, pl.ds(0, widths[k])] = total.reshape(
                n // 2, 2, osh, widths[k])
            stage_copy(k, j + 1).start()

    todo = [(i + 1 + LAG * j, i, j) for i in range(len(steps)) for j in range(nbits - 1)]
    todo.sort()

    def progress(now):
        while todo and todo[0][0] <= now:
            _, i, j = todo.pop(0)
            advance(steps[i][0], steps[i][1], j)

    def halo_wait(q):
        @pl.when(h > 0)
        def _():
            for s in range(nx):
                halo(q, s, True).wait_recv()

        @pl.when(h < ny - 1)
        def _():
            for s in range(nx):
                halo(q, s, False).wait_recv()

    for i, (q, k) in enumerate(steps):
        if k == 0:
            for s in range(1, nx):
                gat[q, s].wait_recv()
                forward(q, s)
        for j, ab in enumerate(CHUNKS[k]):
            if ORDER.index(ab) == 3:
                halo_wait(q)

            def step(p, total, ab=ab, q=q):
                return total + jnp.dot(a3[p], window(q, ab, p), preferred_element_type=f32)
            acc[pl.ds(j * rows, rows)] = lax.fori_loop(
                0, nx, step, jnp.zeros((rows, hc), f32), unroll=nx <= 4)
        used, w = len(CHUNKS[k]) * rows, widths[k]
        if used < w:
            acc[pl.ds(used, w - used)] = jnp.zeros((w - used, hc), f32)
        dwt[q, k, :, :, pl.ds(0, w)] = acc[pl.ds(0, w)].T.reshape(ny // 2, osh, w)

        @pl.when(core != q)
        def _():
            pair_copy(q, k).start()
        progress(i)

    def gi_copy(s):
        return pltpu.make_async_remote_copy(
            src_ref=gsend.at[s], dst_ref=grecv.at[g], send_sem=gi_s.at[s], recv_sem=gi_r.at[s],
            device_id=(xpeer(s), h), device_id_type=MESH)

    def shifted(p):
        def step(ab, total):
            both = jnp.concatenate([window(0, ab, p), window(1, ab, p)], axis=1)
            return total + lax.dot_general(
                wp[pl.ds(3 * ab, 3)].reshape(rows, co), both,
                (((1,), (1,)), ((), ())), preferred_element_type=f32)
        prod = lax.fori_loop(0, 9, step, jnp.zeros((rows, cells), f32))
        low = jnp.where(zpos <= sz - 2, pltpu.roll(prod[:ish], cells - 1, 1), 0.0)
        high = jnp.where(zpos >= 1, pltpu.roll(prod[2 * ish:], 1, 1), 0.0)
        return (prod[ish:2 * ish] + low + high).astype(bf)

    for s in range(1, nx):
        gsend[s] = shifted(xpeer(s))
        gi_copy(s).start()
        progress(len(steps) - 1 + s)
    grecv[g] = shifted(g)
    progress(10 ** 6)

    for s in range(1, nx):
        gi_copy(s).wait_recv()
    full = grecv[...].reshape(nx * ish, cells).astype(f32)
    out_ref[...] = full.T.astype(bf).reshape(sx, sy, sz, nx * ish)
    for k, chunk in enumerate(CHUNKS):
        block = arrived(None, k, nbits - 1)[0] * scale
        for j, ab in enumerate(chunk):
            for c in range(3):
                lane = j * rows + c * ish
                wg_ref[3 * ab + c] = block[:, lane:lane + ish]

    for s in range(1, nx):
        gat[0, s].wait_send()
        gat[1, s].wait_send()
        acts[s].wait_send()
        gi_copy(s).wait_send()

    for q in range(2):
        @pl.when(h < ny - 1)
        def _():
            for s in range(nx):
                halo(q, s, True).wait_send()

        @pl.when(h > 0)
        def _():
            for s in range(nx):
                halo(q, s, False).wait_send()

    for k in range(NCH):
        pair_copy(1 - core, k).wait_send()
        for j in range(1, nbits):
            stage_copy(k, j).wait_send()


def body(nx, ny, grad_out, relu_mask, activations, weight):
    sx, sy, sz, co = grad_out.shape
    ish = weight.shape[1]
    rows = 3 * ish
    cells = sx * sy * sz
    osh = co // ny
    nbits = ny.bit_length() - 1
    assert ny == 2 ** nbits and nbits >= 2
    wide = -(-PER * rows // 128) * 128
    scale = 1.0 / math.sqrt(cells * nx * ny)
    dma = pltpu.SemaphoreType.DMA
    bf, f32 = jnp.bfloat16, jnp.float32
    any_spec = pl.BlockSpec(memory_space=pl.ANY)
    vmem_spec = pl.BlockSpec(memory_space=pltpu.VMEM)
    sizes = [ny // 2 ** (j + 2) for j in range(nbits - 1)]
    out, wg = pl.pallas_call(
        functools.partial(kernel, nx, ny, nbits, scale),
        out_shape=(jax.ShapeDtypeStruct((sx, sy, sz, nx * ish), bf),
                   jax.ShapeDtypeStruct((27, osh, ish), f32)),
        in_specs=[any_spec] * 4,
        out_specs=(vmem_spec, vmem_spec),
        scratch_shapes=[
            pltpu.VMEM((sx, sy, sz, co), bf),
            pltpu.VMEM((sx, sy, sz, co), jnp.int32),
            pltpu.VMEM((sx, sy, sz, nx * ish), bf),
            pltpu.VMEM((2, sx * nx + 2, sy + 2, sz, co // 2), bf),
            pltpu.VMEM((nx, ish, cells), bf),
            pltpu.VMEM((nx, ish, cells), bf),
            pltpu.VMEM((nx, rows, cells), bf),
            pltpu.VMEM((27, ish, co), bf),
            pltpu.VMEM((27, ish, co), bf),
            pltpu.VMEM((wide, co // 2), f32),
            pltpu.VMEM((2, NCH, ny // 2, osh, wide), f32),
            pltpu.VMEM((NCH, ny // 2, osh, wide), f32),
            pltpu.VMEM((nx, ish, cells), bf),
            pltpu.VMEM((nx, ish, cells), bf),
            *[pltpu.VMEM((NCH, n, 2, osh, wide), f32) for n in sizes],
            *[pltpu.VMEM((NCH, n, osh, wide), f32) for n in sizes],
            dma((4,)), dma((2, nx)), dma((2, nx)), dma((nx,)), dma((nx,)),
            dma((2, 2, nx)), dma((2, 2, nx)), dma((NCH,)), dma((NCH,)),
            dma((NCH, nbits)), dma((NCH, nbits)), dma((nx,)), dma((nx,)),
        ],
        compiler_params=pltpu.CompilerParams(
            collective_id=0, has_side_effects=True, vmem_limit_bytes=60 * 1024 * 1024),
        name="conv_backward",
    )(grad_out, relu_mask, activations, weight)
    return out, jnp.transpose(wg, (0, 2, 1))


def solution(mesh):
    nx, ny = mesh.shape["gx"], mesh.shape["gy"]
    in_specs = (
        P("gx", "gy", None, None),
        P("gx", "gy", None, None),
        P("gx", "gy", None, None),
        P(None, "gx", None),
    )
    out_specs = (P("gx", "gy", None, None), P(None, "gx", "gy"))
    return jax.shard_map(
        functools.partial(body, nx, ny), mesh=mesh, in_specs=in_specs, out_specs=out_specs,
        check_vma=False)
```

time: 304 us -> 54.8 us (0.18)
  waiting for transfers between devices: 168 us -> 0 us
  Pallas kernels: 0 us -> 51.5 us
  matrix products: 44.5 us -> 0 us
  local copies, waits for them, and re-layouts: 39 us -> 2.49 us
  starting transfers between devices: 28.2 us -> 0 us
  between operations: 14.6 us -> 0.65 us
  other arithmetic: 7.02 us -> 0 us
    ppermute x8 -> x0, waiting for transfers between devices: 111 us -> none  [the longest x4 99.8 us: padded(): before = lax.ppermute(last, axis, up)]
    pallas_call x0 -> x1, Pallas kernels: none -> 51.5 us  [body(): pl.pallas_call(functools.partial(kernel, nx, ny, nbits, scale), out_shape...]
    dot_general x54 -> x0, matrix products: 44.5 us -> none  [the longest x27 26.5 us: body(): lax.dot_general(shifted, gated_flat, (((0,), (0,)), ((), ())), preferred_...]
    unnamed x3 -> x0, waiting for transfers between devices: 31.3 us -> none
    all_to_all x1 -> x0, waiting for transfers between devices: 26.1 us -> none  [body(): lax.all_to_all(partial_value, 'gy', split_axis=3, concat_axis=0, tiled=True)]
    ppermute x8 -> x0, starting transfers between devices: 23.3 us -> none  [the longest x4 16.6 us: padded(): before = lax.ppermute(last, axis, up)]
    broadcast_in_dim x1 -> x0, local copies, waits for them, and re-layouts: 16.9 us -> none  [body(): partial_value = jnp.stack(terms, axis=0)[None]]
    unnamed x34 -> x4, local copies, waits for them, and re-layouts: 11.5 us -> 2.49 us
  transfers between devices with their start and end apart: 11 -> 0, of which waited for: 7 -> 0; matrix products, arithmetic and copies ran while one was open for 8% -> 0% of each run, Pallas kernels for 0% -> 0%
where the time goes in v2:
time: 54.8 us; the launch traced here: 54.6 us
  Pallas kernels  51.5 us (94%)
  local copies, waits for them, and re-layouts  2.49 us (5%)
  between operations  0.65 us (1%)
    pallas_call x1, Pallas kernels, body(): pl.pallas_call(functools.partial(kernel, nx, ny, nbits, scale), out_shape...  51.5 us
    unnamed x4, local copies, waits for them, and re-layouts  2.49 us

profile of v2, /device:TPU:1, one launch (start us, length us, event | category | flops | bytes accessed | tf_op | source)
XLA Modules:
  0.0 54.6 jit_solution(12846445330517109347)
XLA Ops:
  0.6 51.5 %conv_backward.1 = (bf16[4,2,64,256]{3,2,1,0:T(8,128)(2,1)}, f32[27,32,64]{2,1,0:T(8,128)}) custom-call(bf16[4,2,64,256]{3,2,1,0:T(8,128)(2,1)} %refs_0_.1, s32[4,2,64,256]{3,2,1,0:T(8,128)} %refs_1_.1, bf16[4,2,64,256]{3,2,1,0:T(8,128)(2,1)} %refs_2_.1, bf16[27,64,256]{2,1,0:T(8,128)(2,1)} %refs_3_.1), custom_call_target="tpu_custom_call" | custom-call | tf_op jit(solution)/shard_map/conv_backward/pallas_call | solution.py:306
  52.1 0.0 copy-start
  52.2 1.7 %copy.8 = bf16[4,2,64,256]{3,2,1,0:T(8,128)(2,1)} copy(bf16[4,2,64,256]{3,2,1,0:T(8,128)(2,1)} %get-tuple-element.8) | data formatting | bytes 524288
  53.9 0.0 copy-done
  53.9 0.8 %copy.9 = f32[27,64,32]{1,2,0:T(8,128)} copy(f32[27,64,32]{1,2,0:T(8,128)S(1)} %bitcast.1) | data formatting | bytes 442368
Async XLA Ops:
  52.1 1.7 %copy-start = (f32[27,32,64]{2,1,0:T(8,128)S(1)}, f32[27,32,64]{2,1,0:T(8,128)}, u32[]{:S(2)}) copy-start(f32[27,32,64]{2,1,0:T(8,128)} %get-tuple-element.5) | copy-start | bytes 663556

commit v3 on v1

--- a/solution.py
+++ b/solution.py
@@ -13,13 +13,13 @@
 PER = 2
 
 
-def kernel(nx, ny, scale, gated_ref, act_ref, w_ref, out_ref, wg_ref,
-           gbuf, abuf, a3, wbuf, acc, dwt, pair, red, rs, gsend, grecv,
+def kernel(nx, ny, scale, grad_ref, mask_ref, act_ref, w_ref, out_ref, wg_ref,
+           gin, min_, ain, asend, gbuf, abuf, a3, wbuf, acc, dwt, pair, red, rs, gsend, grecv,
            loc_sem, gat_s, gat_r, act_s, act_r, halo_s, halo_r,
            pair_s, pair_r, rs_s, rs_r, gi_s, gi_r):
     g = lax.axis_index("gx")
     h = lax.axis_index("gy")
-    sx, sy, sz, co = gated_ref.shape
+    sx, sy, sz, co = gin.shape
     ish = w_ref.shape[1]
     rows = 3 * ish
     cells = sx * sy * sz
@@ -38,6 +38,15 @@
     def zpeer(s):
         return 2 * lax.rem(z + s, nz) + core
 
+    in_m = pltpu.make_async_copy(mask_ref, min_, loc_sem.at[0])
+    in_g = pltpu.make_async_copy(grad_ref, gin, loc_sem.at[1])
+    in_a = pltpu.make_async_copy(act_ref, ain, loc_sem.at[2])
+    own_w = pltpu.make_async_copy(w_ref, wbuf, loc_sem.at[3])
+    in_m.start()
+    in_g.start()
+    in_a.start()
+    own_w.start()
+
     barrier = pltpu.get_barrier_semaphore()
     for s in range(1, nx):
         pl.semaphore_signal(barrier, inc=1, device_id=(xpeer(s), h), device_id_type=MESH)
@@ -52,12 +61,14 @@
         pl.semaphore_signal(barrier, inc=1, device_id=(g, outer), device_id_type=MESH)
 
     mine = gbuf.at[pl.ds(1 + sx * g, sx), pl.ds(1, sy)]
-    own_g = pltpu.make_async_copy(gated_ref, mine, loc_sem.at[0])
-    own_a = pltpu.make_async_copy(act_ref.at[g], abuf.at[g], loc_sem.at[1])
-    own_w = pltpu.make_async_copy(w_ref, wbuf, loc_sem.at[2])
-    own_g.start()
-    own_a.start()
-    own_w.start()
+    in_m.wait()
+    in_g.wait()
+    gbuf[pl.ds(1 + sx * g, sx), pl.ds(1, sy)] = jnp.where(
+        min_[...].reshape(cells, co) != 0, gin[...].reshape(cells, co).astype(jnp.float32),
+        0.0).astype(jnp.bfloat16).reshape(sx, sy, sz, co)
+    in_a.wait()
+    asend[...] = ain[...].reshape(cells, nx * ish).astype(jnp.float32).T.astype(
+        jnp.bfloat16).reshape(nx, ish, cells)
     gbuf[0] = jnp.zeros(gbuf.shape[1:], gbuf.dtype)
     gbuf[sx * nx + 1] = jnp.zeros(gbuf.shape[1:], gbuf.dtype)
 
@@ -75,12 +86,12 @@
     acts = {}
     for s in range(1, nx):
         gat[s] = pltpu.make_async_remote_copy(
-            src_ref=gated_ref, dst_ref=mine, send_sem=gat_s.at[s], recv_sem=gat_r.at[s],
+            src_ref=mine, dst_ref=mine, send_sem=gat_s.at[s], recv_sem=gat_r.at[s],
             device_id=(xpeer(s), h), device_id_type=MESH)
         gat[s].start()
     for s in range(1, nx):
         acts[s] = pltpu.make_async_remote_copy(
-            src_ref=act_ref.at[xpeer(s)], dst_ref=abuf.at[g], send_sem=act_s.at[s],
+            src_ref=asend.at[xpeer(s)], dst_ref=abuf.at[g], send_sem=act_s.at[s],
             recv_sem=act_r.at[s], device_id=(xpeer(s), h), device_id_type=MESH)
         acts[s].start()
 
@@ -93,7 +104,6 @@
             src_ref=src, dst_ref=dst, send_sem=halo_s.at[k, s], recv_sem=halo_r.at[k, s],
             device_id=(g, h + 1 if up else h - 1), device_id_type=MESH)
 
-    own_g.wait()
     for s in range(nx):
         if s > 0:
             gat[s].wait_recv()
@@ -108,12 +118,11 @@
 
     lane = lax.broadcasted_iota(jnp.int32, (ish, cells), 1)
     zpos = lax.rem(lane, sz)
-    own_a.wait()
     for s in range(nx):
         if s > 0:
             acts[s].wait_recv()
         p = xfrom(s)
-        v = abuf[p].astype(jnp.float32)
+        v = (abuf[p] if s > 0 else asend[p]).astype(jnp.float32)
         a3[p, pl.ds(0, ish)] = jnp.where(
             zpos >= 1, pltpu.roll(v, 1, 1), 0.0).astype(jnp.bfloat16)
         a3[p, pl.ds(ish, ish)] = v.astype(jnp.bfloat16)
@@ -210,9 +219,11 @@
         for s in range(1, nz):
             rs_copy(k, s, w).wait_recv()
             total = total + rs[k, s, :, pl.ds(0, w)]
-        block = (total * scale).T
+        block = total * scale
         for j, ab in enumerate(chunk):
-            wg_ref[pl.ds(3 * ab, 3)] = block[j * rows:(j + 1) * rows].reshape(3, ish, co // ny)
+            for c in range(3):
+                lane = j * rows + c * ish
+                wg_ref[3 * ab + c] = block[:, lane:lane + ish]
 
     for s in range(1, nx):
         gat[s].wait_send()
@@ -243,8 +254,6 @@
     nz = ny // 2
     nch = -(-9 // PER)
     wide = -(-PER * rows // 128) * 128
-    gated = jnp.where(relu_mask != 0, grad_out, jnp.zeros_like(grad_out))
-    act_t = activations.reshape(cells, nx * ish).T.reshape(nx, ish, cells)
     scale = 1.0 / math.sqrt(cells * nx * ny)
     dma = pltpu.SemaphoreType.DMA
     bf, f32 = jnp.bfloat16, jnp.float32
@@ -253,10 +262,14 @@
     out, wg = pl.pallas_call(
         functools.partial(kernel, nx, ny, scale),
         out_shape=(jax.ShapeDtypeStruct((sx, sy, sz, nx * ish), bf),
-                   jax.ShapeDtypeStruct((27, ish, co // ny), f32)),
-        in_specs=[any_spec] * 3,
+                   jax.ShapeDtypeStruct((27, co // ny, ish), f32)),
+        in_specs=[any_spec] * 4,
         out_specs=(vmem_spec, vmem_spec),
         scratch_shapes=[
+            pltpu.VMEM((sx, sy, sz, co), bf),
+            pltpu.VMEM((sx, sy, sz, co), jnp.int32),
+            pltpu.VMEM((sx, sy, sz, nx * ish), bf),
+            pltpu.VMEM((nx, ish, cells), bf),
             pltpu.VMEM((sx * nx + 2, sy + 2, sz, co), bf),
             pltpu.VMEM((nx, ish, cells), bf),
             pltpu.VMEM((nx, rows, cells), bf),
@@ -268,15 +281,15 @@
             pltpu.VMEM((nch, nz, co // ny, wide), f32),
             pltpu.VMEM((nx, ish, cells), bf),
             pltpu.VMEM((nx, ish, cells), bf),
-            dma((3,)), dma((nx,)), dma((nx,)), dma((nx,)), dma((nx,)),
+            dma((4,)), dma((nx,)), dma((nx,)), dma((nx,)), dma((nx,)),
             dma((2, nx)), dma((2, nx)), dma((nch,)), dma((nch,)),
             dma((nch, nz)), dma((nch, nz)), dma((nx,)), dma((nx,)),
         ],
         compiler_params=pltpu.CompilerParams(
             collective_id=0, has_side_effects=True, vmem_limit_bytes=60 * 1024 * 1024),
         name="conv_backward",
-    )(gated, act_t, weight)
-    return out, wg
+    )(grad_out, relu_mask, activations, weight)
+    return out, jnp.transpose(wg, (0, 2, 1))
 
 
 def solution(mesh):

time: 53.6 us -> 50.2 us (0.937)
  other arithmetic: 1.93 us -> 0 us
  local copies, waits for them, and re-layouts: 3.82 us -> 2.49 us
    pallas_call x1 -> x0, local copies, waits for them, and re-layouts: 2.26 us -> none  [body(): pl.pallas_call(functools.partial(kernel, nx, ny, scale), out_shape=(jax.S...]
    select_n x1 -> x0, other arithmetic: 1.93 us -> none  [body(): gated = jnp.where(relu_mask != 0, grad_out, jnp.zeros_like(grad_out))]
    unnamed x5 -> x4, local copies, waits for them, and re-layouts: 0.71 us -> 2.49 us
    reshape x1 -> x0, local copies, waits for them, and re-layouts: 0.84 us -> none  [body(): act_t = activations.reshape(cells, nx * ish).T.reshape(nx, ish, cells)]
where the time goes in v3:
time: 50.2 us; the launch traced here: 49.8 us
  Pallas kernels  46.7 us (93%)
  local copies, waits for them, and re-layouts  2.49 us (5%)
  between operations  0.65 us (1%)
    pallas_call x1, Pallas kernels, body(): pl.pallas_call(functools.partial(kernel, nx, ny, scale), out_shape=(jax.S...  46.7 us
    unnamed x4, local copies, waits for them, and re-layouts  2.49 us

profile of v3, /device:TPU:1, one launch (start us, length us, event | category | flops | bytes accessed | tf_op | source)
XLA Modules:
  0.0 49.8 jit_solution(17511354762754713415)
XLA Ops:
  0.6 46.7 %conv_backward.1 = (bf16[4,2,64,256]{3,2,1,0:T(8,128)(2,1)}, f32[27,32,64]{2,1,0:T(8,128)}) custom-call(bf16[4,2,64,256]{3,2,1,0:T(8,128)(2,1)} %grad_ref.1, s32[4,2,64,256]{3,2,1,0:T(8,128)} %mask_ref.1, bf16[4,2,64,256]{3,2,1,0:T(8,128)(2,1)} %act_ref.1, bf16[27,64,256]{2,1,0:T(8,128)(2,1)} %w_ref.1), custom_call_target="tpu_custom_call" | custom-call | tf_op jit(solution)/shard_map/conv_backward/pallas_call | solution.py:262
  47.3 0.0 copy-start
  47.3 1.7 %copy.8 = bf16[4,2,64,256]{3,2,1,0:T(8,128)(2,1)} copy(bf16[4,2,64,256]{3,2,1,0:T(8,128)(2,1)} %get-tuple-element.8) | data formatting | bytes 524288
  49.1 0.0 copy-done
  49.1 0.8 %copy.9 = f32[27,64,32]{1,2,0:T(8,128)} copy(f32[27,64,32]{1,2,0:T(8,128)S(1)} %bitcast.1) | data formatting | bytes 442368
Async XLA Ops:
  47.3 1.7 %copy-start = (f32[27,32,64]{2,1,0:T(8,128)S(1)}, f32[27,32,64]{2,1,0:T(8,128)}, u32[]{:S(2)}) copy-start(f32[27,32,64]{2,1,0:T(8,128)} %get-tuple-element.5) | copy-start | bytes 663556
